TPU v7x, 256 devices: a whole 4x4x8 slice. The times are simulated.
256 devices in a mesh: row: 16 (over x, y_hi, core), col: 16 (over z, y_lo).
Axes of the slice: x: 4, y: 4 (y_hi: 2, y_lo: 2; y = y_hi * 2 + y_lo), z: 8, core: 2. Of those that a mesh axis runs over, the one named last changes fastest.
Arguments:
- record: float32 [2, 262144], P(None, ('row', 'col')), may hold values from -5 to 5
Outputs:
- spectrum: float32 [256, 256, 16, 2, 256], P('row', 'col')
All inputs are finite; a program needn't handle non-finite values.
Results may differ from a plain program's by a relative error of at most 0.00011.
Values sent between devices are 32-bit elements; how exact they have to be, the bound alone decides.
A program may use at most 64 MiB of HBM per device.

v0:
```python
import math

import jax
import jax.numpy as jnp
from jax import lax
from jax.sharding import PartitionSpec as P

C = 256
P_SIZE = 256
HOP = 64


highest = lax.Precision.HIGHEST


def passed_along(block, axis, distance):
    devices = range(lax.axis_size(axis))
    route = [(i - distance, i) for i in devices if i - distance in devices]
    return lax.ppermute(block, axis, route)


def copy_for_each(value, axis):
    length = lax.axis_size(axis)
    return lax.all_to_all(
        jnp.broadcast_to(value[None], (length, *value.shape)), axis, 0, 0, tiled=True
    )


def in_order(blocks, dim):
    blocks = jnp.moveaxis(blocks, 0, dim)
    lengths = blocks.shape
    return blocks.reshape(*lengths[:dim], lengths[dim] * lengths[dim + 1], *lengths[dim + 2 :])


def collect(value, axis, dim):
    blocks = copy_for_each(value, axis)
    return in_order(blocks, dim)


def spectral_table(length, start_column, width, weights):
    position = jnp.arange(length, dtype=jnp.int32)
    column = start_column + jnp.arange(width, dtype=jnp.int32)
    turns = position[:, None] * column[None, :] % length
    phase = turns.astype(jnp.float32) * (2.0 * math.pi / length)
    cosine = weights[:, None] * jnp.cos(phase)
    sinus = weights[:, None] * jnp.sin(phase)
    upper = jnp.stack([cosine, -sinus], axis=1)
    bottom = jnp.stack([sinus, cosine], axis=1)
    return jnp.stack([upper, bottom], axis=0)


def hann_weights():
    position = jnp.arange(C, dtype=jnp.int32).astype(jnp.float32)
    return (0.5 - 0.5 * jnp.cos(position * (2.0 * math.pi / C))) / math.sqrt(3.0 * C / 8.0)


def framed(samples, amount):
    blocks = samples.reshape(2, amount + C // HOP - 1, HOP)
    return jnp.concatenate(
        [blocks[:, offset : offset + amount] for offset in range(C // HOP)], axis=2
    )


def downconvert(spectra, start_channel, start_frame):
    channel = start_channel + jnp.arange(spectra.shape[1], dtype=jnp.int32)
    moment = start_frame + jnp.arange(spectra.shape[2], dtype=jnp.int32)
    turns = (channel * HOP % C)[:, None] * (moment % C)[None, :] % C
    phase = turns.astype(jnp.float32) * (2.0 * math.pi / C)
    cosine = jnp.cos(phase)
    sinus = jnp.sin(phase)
    real_part = spectra[0] * cosine + spectra[1] * sinus
    imag_part = spectra[1] * cosine - spectra[0] * sinus
    return jnp.stack([real_part, imag_part])


def channelize(frames, start_channel, width, start_frame):
    weights = spectral_table(C, start_channel, width, hann_weights())
    spectra = lax.dot_general(
        weights,
        frames,
        (((0, 1), (0, 2)), ((), ())),
        precision=highest,
        preferred_element_type=jnp.float32,
    )
    return downconvert(spectra, start_channel, start_frame)


def correlate(leading, trailing):
    lead_count = leading.shape[1]
    trail_count = trailing.shape[1]
    windows = leading.shape[2] // P_SIZE
    lead = leading.reshape(2, lead_count, windows, P_SIZE)
    trail = trailing.reshape(2, trail_count, windows, P_SIZE)
    real_part = lead[0][:, None] * trail[0][None] + lead[1][:, None] * trail[1][None]
    imag_part = lead[1][:, None] * trail[0][None] - lead[0][:, None] * trail[1][None]
    weights = spectral_table(
        P_SIZE, 0, P_SIZE, jnp.full((P_SIZE,), 1.0 / math.sqrt(P_SIZE), jnp.float32)
    )
    real_table = weights[0].reshape(P_SIZE, 2 * P_SIZE)
    imag_table = weights[1].reshape(P_SIZE, 2 * P_SIZE)
    dims = (((3,), (0,)), ((), ()))
    result = lax.dot_general(
        real_part, real_table, dims, precision=highest, preferred_element_type=jnp.float32
    )
    result = result + lax.dot_general(
        imag_part, imag_table, dims, precision=highest, preferred_element_type=jnp.float32
    )
    return result.reshape(lead_count, trail_count, windows, 2, P_SIZE)


def local(record):
    row_count = lax.axis_size("row")
    col_count = lax.axis_size("col")
    lead_width = C // row_count
    trail_width = C // col_count
    own_frames = record.shape[1] // HOP
    device = lax.axis_index("row") * col_count + lax.axis_index("col")
    follow = passed_along(record[:, : C - HOP], ("row", "col"), -1)
    frames = framed(jnp.concatenate([record, follow], axis=1), own_frames)
    spectra = channelize(frames, 0, C, device * own_frames)
    shaped = spectra.reshape(2, C, 1, 1, own_frames)
    leading = lax.all_to_all(shaped, "row", split_axis=1, concat_axis=2, tiled=True)
    leading = collect(leading, "col", 3)
    trailing = lax.all_to_all(shaped, "col", split_axis=1, concat_axis=3, tiled=True)
    trailing = collect(trailing, "row", 2)
    leading = leading.reshape(2, lead_width, -1)
    trailing = trailing.reshape(2, trail_width, -1)
    return correlate(leading, trailing)


def solution(mesh):
    return jax.shard_map(
        local,
        mesh=mesh,
        in_specs=(P(None, ("row", "col")),),
        out_specs=P("row", "col", None, None, None),
        check_vma=False,
    )
```

profile of v0, /device:TPU:1, one launch (start us, length us, event | category | flops | bytes accessed | tf_op | source)
XLA Modules:
  0.0 127.3 jit_solution(5578078912147120790)
XLA Ops:
  0.0 0.7 slice.43
  0.7 9.9 %collective-permute-start = (f32[2,192]{1,0:T(2,128)S(1)}, f32[2,192]{1,0:T(2,128)S(1)}, u32[]{:S(2)}, u32[]{:S(2)}) collective-permute-start(f32[2,192]{1,0:T(2,128)S(1)} %slice.43), channel_id=1, source_target_pairs={{1,0},{2,1},{3,2},{4,3},{5,4},{6,5},{7,6},{8,7},{9,8},{10,9},{11,1... | collective-permute-start | bytes 4616 | tf_op jit(solution)/shard_map/ppermute | solution.py:19
  10.6 1.1 fusion.33
  11.7 0.1 maximum_bitcast_fusion
  11.8 0.0 collective-permute-done
  11.8 0.7 pad_maximum_fusion.2
  12.5 0.1 reshape.356
  12.6 0.7 convolution_bitcast_fusion
  13.3 0.2 multiply_add_fusion
  13.5 0.1 copy.24
  13.6 1.0 reshape.363
  14.6 4.9 %all-to-all-start.2 = ((f32[16,1,512]{2,1,0:T(1,128)}), f32[16,1,512]{2,1,0:T(1,128)S(1)}, u32[]{:S(2)}, u32[]{:S(2)}) async-start(f32[16,1,512]{2,1,0:T(1,128)} %reshape.363), calls=%async_computation.2 | async-start | bytes 65536 | tf_op jit(solution)/shard_map/all_to_all | solution.py:124
  19.5 0.9 reshape.367
  20.5 6.7 %all-to-all-done.2 = f32[16,1,512]{2,1,0:T(1,128)S(1)} async-done(((f32[16,1,512]{2,1,0:T(1,128)}), f32[16,1,512]{2,1,0:T(1,128)S(1)}, u32[]{:S(2)}, u32[]{:S(2)}) %all-to-all-start.2) | async-done | bytes 32800 | tf_op jit(solution)/shard_map/all_to_all | solution.py:124
  27.1 9.4 %all-to-all-start = ((f32[16,1,512]{2,1,0:T(1,128)}), f32[16,1,512]{2,1,0:T(1,128)S(1)}, u32[]{:S(2)}, u32[]{:S(2)}) async-start(f32[16,1,512]{2,1,0:T(1,128)} %reshape.367), calls=%async_computation | async-start | bytes 65536 | tf_op jit(solution)/shard_map/all_to_all | solution.py:122
  36.6 0.6 broadcast.535
  37.1 0.7 reduce
  37.9 0.4 reshape.364
  38.3 0.2 copy.28
  38.4 2.5 %broadcast_bitcast_fusion = f32[16,2,1,16,16,16]{5,4,3,2,1,0:T(8,128)} fusion(f32[2,16,16,16]{3,2,1,0:T(8,128)S(1)} %copy.28), kind=kLoop, calls=%fused_computation.78 | loop fusion | bytes 557056
  40.9 4.2 %reshape.365 = f32[16,1,8192]{2,1,0:T(1,128)} reshape(f32[16,2,1,16,16,16]{5,4,3,2,1,0:T(8,128)} %broadcast_bitcast_fusion) | data formatting | bytes 1048576
  45.1 0.0 all-to-all-done
  45.1 7.2 %all-to-all-start.3 = ((f32[16,1,8192]{2,1,0:T(1,128)}), f32[16,1,8192]{2,1,0:T(1,128)S(1)}, u32[]{:S(2)}, u32[]{:S(2)}) async-start(f32[16,1,8192]{2,1,0:T(1,128)} %reshape.365), calls=%async_computation.3 | async-start | bytes 1048576 | tf_op jit(solution)/shard_map/all_to_all | solution.py:24
  52.3 1.1 broadcast_multiply_fusion
  53.4 0.7 reduce.2
  54.1 0.4 reshape.368
  54.5 0.2 copy.25
  54.7 2.5 %broadcast_bitcast_fusion.1 = f32[16,2,1,16,16,16]{5,4,3,2,1,0:T(8,128)} fusion(f32[2,16,16,16]{3,2,1,0:T(8,128)S(1)} %copy.25), kind=kLoop, calls=%fused_computation.79 | loop fusion | bytes 557056
  57.1 4.2 %reshape.369 = f32[16,1,8192]{2,1,0:T(1,128)} reshape(f32[16,2,1,16,16,16]{5,4,3,2,1,0:T(8,128)} %broadcast_bitcast_fusion.1) | data formatting | bytes 1048576
  61.3 2.2 %all-to-all-done.3 = f32[16,1,8192]{2,1,0:T(1,128)S(1)} async-done(((f32[16,1,8192]{2,1,0:T(1,128)}), f32[16,1,8192]{2,1,0:T(1,128)S(1)}, u32[]{:S(2)}, u32[]{:S(2)}) %all-to-all-start.3) | async-done | bytes 524320 | tf_op jit(solution)/shard_map/all_to_all | solution.py:24
  63.5 3.8 %all-to-all-start.1 = ((f32[16,1,8192]{2,1,0:T(1,128)}), f32[16,1,8192]{2,1,0:T(1,128)S(1)}, u32[]{:S(2)}, u32[]{:S(2)}) async-start(f32[16,1,8192]{2,1,0:T(1,128)} %reshape.369), calls=%async_computation.1 | async-start | bytes 1048576 | tf_op jit(solution)/shard_map/all_to_all | solution.py:24
  67.3 1.0 fusion.32
  68.3 0.1 pad_maximum_fusion
  68.4 1.0 copy.32
  69.4 1.0 copy.34
  70.4 1.9 %reduce.1 = f32[16,8192]{1,0:T(8,128)S(1)} reduce(f32[16,1,8192]{2,1,0:T(1,128)S(1)} %all-to-all-done.3, f32[]{:T(128)} %broadcast.535), dimensions={1}, to_apply=%all_to_all.35.reduce_sub_computation | reduce | bytes 1048580 | tf_op jit(solution)/shard_map/all_to_all | solution.py:24
  72.2 2.8 %reshape.366 = f32[16,2,1,16,16,16]{5,4,3,2,1,0:T(8,128)} reshape(f32[16,8192]{1,0:T(8,128)S(1)} %reduce.1) | data formatting | bytes 1048576
  75.0 2.5 %bitcast_bitcast_fusion.1 = f32[2,16,16,1,16,16]{5,4,1,3,0,2:T(8,128)S(1)} fusion(f32[16,2,1,16,16,16]{5,4,3,2,1,0:T(8,128)} %reshape.366), kind=kLoop, calls=%fused_computation.77 | loop fusion | bytes 1048576 | tf_op jit(solution)/shard_map/transpose | solution.py:30
  77.6 1.7 %fusion.49 = (f32[1,16,16,1,16,16]{5,4,1,3,0,2:T(8,128)}, f32[1,16,16,1,16,16]{5,4,1,3,0,2:T(8,128)S(1)}) fusion(f32[2,16,16,1,16,16]{5,4,1,3,0,2:T(8,128)S(1)} %bitcast_bitcast_fusion.1), kind=kLoop, calls=%fused_computation.74 | loop fusion | bytes 1048576 | tf_op jit(solution)/shard_map/slice | solution.py:94
  79.3 2.4 %mul.355 = f32[16,16,256]{2,0,1:T(8,128)S(1)} reshape(f32[1,16,16,1,16,16]{5,4,1,3,0,2:T(8,128)} %get-tuple-element.7) | data formatting | bytes 524288 | tf_op jit(solution)/shard_map/mul | solution.py:94
  81.7 0.2 copy.29
  81.9 0.9 mul.360
  82.8 0.2 copy.31
  83.0 0.0 all-to-all-done.1
  83.0 1.9 %reduce.3 = f32[16,8192]{1,0:T(8,128)S(1)} reduce(f32[16,1,8192]{2,1,0:T(1,128)S(1)} %all-to-all-done.1, f32[]{:T(128)} %broadcast.535), dimensions={1}, to_apply=%all_to_all.31.reduce_sub_computation | reduce | bytes 1048580 | tf_op jit(solution)/shard_map/all_to_all | solution.py:24
  84.9 2.8 %reshape.370 = f32[16,2,1,16,16,16]{5,4,3,2,1,0:T(8,128)} reshape(f32[16,8192]{1,0:T(8,128)S(1)} %reduce.3) | data formatting | bytes 1048576
  87.7 2.5 %bitcast_bitcast_fusion = f32[2,16,16,16,1,16]{5,2,1,4,0,3:T(8,128)S(1)} fusion(f32[16,2,1,16,16,16]{5,4,3,2,1,0:T(8,128)} %reshape.370), kind=kLoop, calls=%fused_computation.76 | loop fusion | bytes 1048576 | tf_op jit(solution)/shard_map/transpose | solution.py:30
  90.2 1.7 %fusion.48 = (f32[1,16,16,16,1,16]{5,2,1,4,0,3:T(8,128)S(1)}, f32[1,16,16,16,1,16]{5,2,1,4,0,3:T(8,128)}) fusion(f32[2,16,16,16,1,16]{5,2,1,4,0,3:T(8,128)S(1)} %bitcast_bitcast_fusion), kind=kLoop, calls=%fused_computation.73 | loop fusion | bytes 1048576 | tf_op jit(solution)/shard_map/slice | solution.py:94
  91.9 1.2 copy.26
  93.2 0.9 mul.353
  94.1 2.8 %copy.30 = f32[1,16,16,16,1,16]{5,3,2,1,4,0:T(8,128)S(1)} copy(f32[1,16,16,16,1,16]{5,2,1,4,0,3:T(8,128)} %get-tuple-element.6) | data formatting | bytes 524288 | tf_op jit(solution)/shard_map/slice | solution.py:94
  96.9 0.9 mul.358
  97.8 0.0 copy-start
  97.8 9.1 %fusion = f32[16,16,16,512]{3,2,1,0:T(8,128)S(1)} fusion(f32[256,512,1,1]{0,1,3,2:T(8,128)} %bitcast.69, f32[16,16,256]{2,1,0:T(8,128)S(1)} %copy.31, f32[16,16,256]{2,1,0:T(8,128)S(1)} %mul.358, f32[16,16,256]{2,1,0:T(8,128)S(1)} %copy.29, f32[16,16,256]{2,1,0:T(8,128)S(1)} %mul.353), kind=kOutput, calls=%fused_computation | convolution fusion | flops 6445596672 | bytes 9961472 | tf_op jit(solution)/shard_map/dot_general | solution.py:105
  107.2 0.0 copy-done
  107.2 9.6 %fusion.8 = f32[16,16,16,512]{3,2,1,0:T(8,128)} fusion(f32[16,16,16,512]{3,2,1,0:T(8,128)S(1)} %fusion, f32[256,512,1,1]{0,1,3,2:T(8,128)S(1)} %bitcast.68, f32[16,16,256]{2,1,0:T(8,128)S(1)} %copy.31, f32[16,16,256]{2,1,0:T(8,128)S(1)} %mul.358, f32[16,16,256]{2,1,0:T(8,128)S(1)} %copy.29, f32[16,16,256]{2,1,0:T(8,128)S(1)} %mul.353), kind=kOutput, calls=%fused_computation.8 | convolution fusion | flops 6447693824 | bytes 18350080 | tf_op jit(solution)/shard_map/dot_general | solution.py:102
  116.8 10.5 %reshape.358 = f32[16,16,16,2,256]{4,3,2,1,0:T(2,128)} reshape(f32[16,16,16,512]{3,2,1,0:T(8,128)} %fusion.8) | data formatting | bytes 16777216 | tf_op jit(solution)/shard_map/reshape | solution.py:108
  (5 shorter events, 0.1 us)
Async XLA Ops:
  0.7 11.1 %collective-permute-start = (f32[2,192]{1,0:T(2,128)S(1)}, f32[2,192]{1,0:T(2,128)S(1)}, u32[]{:S(2)}, u32[]{:S(2)}) collective-permute-start(f32[2,192]{1,0:T(2,128)S(1)} %slice.43), channel_id=1, source_target_pairs={{1,0},{2,1},{3,2},{4,3},{5,4},{6,5},{7,6},{8,7},{9,8},{10,9},{11,1... | collective-permute-start | bytes 4616 | tf_op jit(solution)/shard_map/ppermute | solution.py:19
  14.6 12.6 %all-to-all-start.2 = ((f32[16,1,512]{2,1,0:T(1,128)}), f32[16,1,512]{2,1,0:T(1,128)S(1)}, u32[]{:S(2)}, u32[]{:S(2)}) async-start(f32[16,1,512]{2,1,0:T(1,128)} %reshape.363), calls=%async_computation.2 | async-start | bytes 65536 | tf_op jit(solution)/shard_map/all_to_all | solution.py:124
  27.1 18.0 %all-to-all-start = ((f32[16,1,512]{2,1,0:T(1,128)}), f32[16,1,512]{2,1,0:T(1,128)S(1)}, u32[]{:S(2)}, u32[]{:S(2)}) async-start(f32[16,1,512]{2,1,0:T(1,128)} %reshape.367), calls=%async_computation | async-start | bytes 65536 | tf_op jit(solution)/shard_map/all_to_all | solution.py:122
  45.1 18.4 %all-to-all-start.3 = ((f32[16,1,8192]{2,1,0:T(1,128)}), f32[16,1,8192]{2,1,0:T(1,128)S(1)}, u32[]{:S(2)}, u32[]{:S(2)}) async-start(f32[16,1,8192]{2,1,0:T(1,128)} %reshape.365), calls=%async_computation.3 | async-start | bytes 1048576 | tf_op jit(solution)/shard_map/all_to_all | solution.py:24
  63.5 19.5 %all-to-all-start.1 = ((f32[16,1,8192]{2,1,0:T(1,128)}), f32[16,1,8192]{2,1,0:T(1,128)S(1)}, u32[]{:S(2)}, u32[]{:S(2)}) async-start(f32[16,1,8192]{2,1,0:T(1,128)} %reshape.369), calls=%async_computation.1 | async-start | bytes 1048576 | tf_op jit(solution)/shard_map/all_to_all | solution.py:24
  97.8 9.3 %copy-start = (f32[256,2,256]{0,2,1:T(8,128)S(1)}, f32[256,2,256]{0,2,1:T(8,128)}, u32[]{:S(2)}) copy-start(f32[256,2,256]{0,2,1:T(8,128)} %copy.32) | copy-start | bytes 1572868
where the time goes:
time: 129 us; the launch traced here: 127 us
  local copies, waits for them, and re-layouts  54 us (42%)
  starting transfers between devices  35.2 us (27%)
  matrix products  19.3 us (15%)
  other arithmetic  9.37 us (7%)
  waiting for transfers between devices  8.88 us (7%)
    unnamed x12, local copies, waits for them, and re-layouts  21.6 us
    all_to_all x2, starting transfers between devices, copy_for_each(): lax.all_to_all(jnp.broadcast_to(value[None], (length, *value.shape)), axi...  11 us
    reshape x1, local copies, waits for them, and re-layouts, correlate(): return result.reshape(lead_count, trail_count, windows, 2, P_SIZE)  10.5 us
    ppermute x1, starting transfers between devices, passed_along(): return lax.ppermute(block, axis, route)  9.86 us
    dot_general x1, matrix products, correlate(): lax.dot_general(real_part, real_table, dims, precision=highest, preferred...  9.6 us
    all_to_all x1, starting transfers between devices, local(): lax.all_to_all(shaped, 'row', split_axis=1, concat_axis=2, tiled=True)  9.44 us
    dot_general x1, matrix products, correlate(): lax.dot_general(imag_part, imag_table, dims, precision=highest, preferred...  9.07 us
    all_to_all x1, waiting for transfers between devices, local(): lax.all_to_all(shaped, 'col', split_axis=1, concat_axis=3, tiled=True)  6.68 us
  transfers between devices with their start and end apart: 5, of which 2 were waited for; matrix products, arithmetic and copies ran while one was open for 28% of the time, Pallas kernels for 0%

commit v1 on v0

v1 whole, which is shorter than its diff:
```python
import math

import jax
import jax.numpy as jnp
import numpy as np
from jax import lax
from jax.experimental import pallas as pl
from jax.experimental.pallas import tpu as pltpu
from jax.sharding import PartitionSpec as P

C = 256
P_SIZE = 256
HOP = 64
LANES = 128
WIDTH = 16
WINDOWS = 16
ROWS = 2048
PIECES = 3
DEPTH = PIECES * 2 * LANES


def channel_tables():
    position = np.arange(PIECES * LANES)
    table = np.zeros((PIECES, 2, LANES, 2, 2, WIDTH))
    turned = np.zeros_like(table)
    for parity in range(2):
        m = position - HOP * parity
        inside = (m >= 0) & (m < C)
        hann = np.where(inside, (0.5 - 0.5 * np.cos(2 * np.pi * m / C)) / math.sqrt(3 * C / 8), 0.0)
        turns = (position[:, None] * np.arange(WIDTH)[None]) % C
        w = hann[:, None] * np.exp(-2j * np.pi * turns / C)
        for part, v in enumerate((w, 1j * w)):
            v = v.reshape(PIECES, LANES, WIDTH)
            table[:, part, :, parity, 0] = v.real
            table[:, part, :, parity, 1] = v.imag
            turned[:, part, :, parity, 0] = v.imag
            turned[:, part, :, parity, 1] = -v.real
    tables = np.stack([table, turned]).reshape(2, DEPTH, 64)
    tables = np.concatenate([tables, tables], axis=2)
    angle = 2 * np.pi * (np.arange(16)[:, None] * np.arange(16)[None] % 16) / 16
    turns = np.stack([np.cos(angle), np.sin(angle)])
    turns = np.broadcast_to(turns[..., None], (2, 16, 16, LANES))
    return tables.astype(np.float32), np.ascontiguousarray(turns).astype(np.float32)


def second_tables():
    frame = np.arange(LANES)
    bins = np.arange(LANES)
    out = []
    for parity in range(2):
        turns = ((2 * frame[:, None] + parity) * bins[None]) % P_SIZE
        angle = 2 * np.pi * turns / P_SIZE
        c, s = np.cos(angle) / 16.0, np.sin(angle) / 16.0
        out.append(np.concatenate([np.concatenate([c, -s], 1), np.concatenate([s, c], 1)], 0))
    full = np.stack(out).astype(np.float32)
    high = full.astype(jnp.bfloat16)
    low = (full - high.astype(np.float32)).astype(jnp.bfloat16)
    return np.stack([high, low])


def signs():
    channel = np.arange(LANES) % WIDTH
    frame = np.arange(LANES)
    return np.where((channel[:, None] * frame[None]) % 2 == 1, -1.0, 1.0).astype(np.float32)


def halves(value):
    high = value.astype(jnp.bfloat16)
    low = (value - high.astype(jnp.float32)).astype(jnp.bfloat16)
    return high, low


def dot(a, b):
    return lax.dot_general(a, b, (((1,), (0,)), ((), ())), preferred_element_type=jnp.float32)


def channelize(gathered, tables, turns, sign, base):
    row = lax.axis_index("row")
    col = lax.axis_index("col")
    lane = lax.broadcasted_iota(jnp.int32, (16, LANES), 1)
    cosine = jnp.where(lane < 64, turns[0, row], turns[0, col])
    sinus = jnp.where(lane < 64, turns[1, row], turns[1, col])
    groups = DEPTH // 16
    shaped = tables[...].reshape(2, groups, 16, LANES)
    weights = (shaped[0] * cosine[None] + shaped[1] * sinus[None]).reshape(DEPTH, LANES)
    high_w, low_w = halves(weights)
    both = jnp.concatenate([high_w, low_w], axis=1)
    step = 512

    def block(i, _):
        start = pl.multiple_of(i * (2 * step), 2 * step)
        pieces = [gathered[pl.ds(start + j, step, stride=2), :] for j in range(2 * PIECES)]
        high, low = halves(jnp.concatenate(pieces, axis=1))
        wide = dot(high, both)
        result = wide[:, :LANES] + wide[:, LANES:] + dot(low, high_w)
        for k in range(step // LANES):
            turned = result[k * LANES : (k + 1) * LANES].T * sign[...]
            base[pl.ds(i * (step // LANES) + k, LANES, stride=WINDOWS), :] = turned
        return 0

    lax.fori_loop(0, ROWS // step, block, 0)


def correlate(a, base, second, out):
    def tile(first, count):
        return base[pl.ds(pl.multiple_of(first * WINDOWS, WINDOWS), count * WINDOWS), :]

    sums = []
    for parity in range(2):
        lead_re = tile(parity * 32 + a, 1)[None]
        lead_im = tile(parity * 32 + 16 + a, 1)[None]
        trail_re = tile(64 + parity * 32, 16).reshape(WIDTH, WINDOWS, LANES)
        trail_im = tile(64 + parity * 32 + 16, 16).reshape(WIDTH, WINDOWS, LANES)
        real = (lead_re * trail_re + lead_im * trail_im).reshape(256, LANES)
        imag = (lead_im * trail_re - lead_re * trail_im).reshape(256, LANES)
        high, low = halves(jnp.concatenate([real, imag], axis=1))
        sums.append(dot(high, second[0, parity]) + dot(low, second[0, parity]) + dot(high, second[1, parity]))
    total = sums[0] + sums[1]
    rest = sums[0] - sums[1]
    for j, value in enumerate((total[:, :LANES], total[:, LANES:], rest[:, :LANES], rest[:, LANES:])):
        out[pl.ds(j, 256, stride=4), :] = value


def kernel(gathered, tables, turns, sign, second, out, padded, base):
    a = pl.program_id(0)

    @pl.when(a == 0)
    def _():
        padded[0 : 2 * ROWS, :] = gathered[...]
        padded[2 * ROWS :, :] = jnp.zeros((8, LANES), jnp.float32)
        channelize(padded, tables, turns, sign, base)

    correlate(a, base, second, out)


def spectra(gathered):
    tables, turns = channel_tables()

    def whole(shape):
        return pl.BlockSpec(shape, lambda a: (0,) * len(shape), pipeline_mode=pl.Buffered(1))

    return pl.pallas_call(
        kernel,
        grid=(WIDTH,),
        out_shape=jax.ShapeDtypeStruct((WIDTH * 1024, LANES), jnp.float32),
        in_specs=[
            whole((2 * ROWS, LANES)),
            whole((2, DEPTH, LANES)),
            whole((2, 16, 16, LANES)),
            whole((LANES, LANES)),
            whole((2, 2, 256, 256)),
        ],
        out_specs=pl.BlockSpec((1024, LANES), lambda a: (a, 0)),
        scratch_shapes=[
            pltpu.VMEM((2 * ROWS + 8, LANES), jnp.float32),
            pltpu.VMEM((LANES * WINDOWS, LANES), jnp.float32),
        ],
        compiler_params=pltpu.CompilerParams(dimension_semantics=("arbitrary",)),
    )(gathered, jnp.asarray(tables), jnp.asarray(turns), jnp.asarray(signs()), jnp.asarray(second_tables()))


def local(record):
    tiles = record.reshape(2, 8, LANES).transpose(1, 0, 2).reshape(16, LANES)
    gathered = lax.all_gather(tiles, ("row", "col"), axis=0, tiled=True)
    result = spectra(gathered)
    result = result.reshape(WIDTH, WIDTH, WINDOWS, 2, 2, LANES)
    result = result.transpose(0, 1, 2, 4, 3, 5)
    return result.reshape(WIDTH, WIDTH, WINDOWS, 2, 2 * LANES)


def solution(mesh):
    return jax.shard_map(
        local,
        mesh=mesh,
        in_specs=(P(None, ("row", "col")),),
        out_specs=P("row", "col", None, None, None),
        check_vma=False,
    )
```

time: 129 us -> 753 us (5.84)
  waiting for transfers between devices: 8.88 us -> 722 us
  local copies, waits for them, and re-layouts: 54 us -> 0 us
  starting transfers between devices: 35.2 us -> 0.01 us
  matrix products: 19.3 us -> 0 us
  Pallas kernels: 0 us -> 14.9 us
  between operations: 0.49 us -> 13.4 us
  other arithmetic: 9.37 us -> 0 us
    all_gather x0 -> x1, waiting for transfers between devices: none -> 721 us  [local(): gathered = lax.all_gather(tiles, ('row', 'col'), axis=0, tiled=True)]
    all_to_all x4 -> x0, starting transfers between devices: 25.3 us -> none  [the longest x2 11 us: copy_for_each(): lax.all_to_all(jnp.broadcast_to(value[None], (length, *value.shape)), axi...]
    unnamed x12 -> x0, local copies, waits for them, and re-layouts: 21.6 us -> none
    dot_general x3 -> x0, matrix products: 19.3 us -> none  [the longest x1 9.6 us: correlate(): lax.dot_general(real_part, real_table, dims, precision=highest, preferred...]
    pallas_call x0 -> x1, Pallas kernels: none -> 14.9 us  [spectra(): pl.pallas_call(kernel, grid=(WIDTH,), out_shape=jax.ShapeDtypeStruct((WID...]
    reshape x3 -> x0, local copies, waits for them, and re-layouts: 10.8 us -> none  [the longest x1 10.5 us: correlate(): return result.reshape(lead_count, trail_count, windows, 2, P_SIZE)]
    ppermute x1 -> x0, starting transfers between devices: 9.86 us -> none  [passed_along(): return lax.ppermute(block, axis, route)]
    all_to_all x4 -> x0, waiting for transfers between devices: 8.88 us -> none  [the longest x1 6.68 us: local(): lax.all_to_all(shaped, 'col', split_axis=1, concat_axis=3, tiled=True)]
  transfers between devices with their start and end apart: 5 -> 1, of which waited for: 2 -> 1; matrix products, arithmetic and copies ran while one was open for 28% -> 0% of each run, Pallas kernels for 0% -> 0%
where the time goes in v1:
time: 753 us; the launch traced here: 750 us
  waiting for transfers between devices  722 us (96%)
  Pallas kernels  14.9 us (2%)
  between operations  13.4 us (2%)
    all_gather x1, waiting for transfers between devices, local(): gathered = lax.all_gather(tiles, ('row', 'col'), axis=0, tiled=True)  721 us
  transfers between devices with their start and end apart: 1, of which 1 were waited for; matrix products, arithmetic and copies ran while one was open for 0% of the time, Pallas kernels for 0%

profile of v1, /device:TPU:1, one launch (start us, length us, event | category | flops | bytes accessed | tf_op | source)
XLA Modules:
  0.0 750.1 jit_solution(12904243134358017560)
XLA Ops:
  6.5 0.0 all-gather.2.cloned.1.call-start
  6.5 0.7 all-gather.2.cloned.1.call-update
  7.3 721.1 %all-gather.2.cloned.1.call-done.gathered = f32[4096,128]{1,0:T(8,128)} async-done(((f32[16,128]{1,0:T(8,128)}), f32[4096,128]{1,0:T(8,128)}) %all-gather.2.cloned.1.call-update) | async-done | bytes 2097168 | tf_op jit(solution)/shard_map/all_gather | solution.py:164
  728.4 14.9 %shard_map.55 = f32[16384,128]{1,0:T(8,128)} custom-call(f32[4096,128]{1,0:T(8,128)} %all-gather.2.cloned.1.call-done.gathered, f32[2,768,128]{2,1,0:T(8,128)} %constant.8.clone.tables, f32[2,16,16,128]{3,2,1,0:T(8,128)} %constant.9.clone.turns, f32[128,128]{1,0:T(8,128)} %constant.10.clone.sign, bf16[2,2,256,256]{3,2,1,0:T(8,128)(2,1)} %constant.11.clone.second), custom_call_target="tpu_custom_call" | custom-call | tf_op jit(solution)/shard_map/pallas_call | solution.py:142
Async XLA Ops:
  6.5 721.9 %all-gather.2.cloned.1.call-start = ((), (), s32[]{:S(2)}) async-start(), calls=%async_computation | async-start | bytes 2105344 | tf_op jit(solution)/shard_map/all_gather | solution.py:164
Sparse Core Ops, SparseCore 0:
  9.2 719.1 all-gather.1

commit v2 on v1

--- a/solution.py
+++ b/solution.py
@@ -159,9 +159,144 @@
     )(gathered, jnp.asarray(tables), jnp.asarray(turns), jnp.asarray(signs()), jnp.asarray(second_tables()))
 
 
+MESH = pl.DeviceIdType.MESH
+PLUS = (0, 1)
+
+
+def gather_kernel(own, out, copied, z_send, z_recv, far_send, far_recv, near_send, near_recv, core_send, core_recv):
+    row = lax.axis_index("row")
+    col = lax.axis_index("col")
+    core = lax.rem(row, 2)
+    x = lax.div(row, 4)
+    y = lax.rem(lax.div(row, 2), 2) * 2 + lax.rem(col, 2)
+    z = lax.div(col, 2)
+
+    def device(x, y, z, core):
+        return (x * 4 + lax.div(y, 2) * 2 + core, z * 2 + lax.rem(y, 2))
+
+    def moved(value, distance, length=4):
+        return lax.rem(value + (distance + length), length)
+
+    def piece(half, x, y):
+        return out.at[x, lax.div(y, 2), core, pl.ds(4 * half, 4), lax.rem(y, 2)]
+
+    started = []
+
+    def send(source, target, send_sem, recv_sem, to):
+        copy = pltpu.make_async_remote_copy(
+            src_ref=source, dst_ref=target, send_sem=send_sem, recv_sem=recv_sem, device_id=to, device_id_type=MESH
+        )
+        copy.start()
+        started.append(copy)
+
+    def arrived(ref, recv_sem):
+        pltpu.make_async_copy(ref, ref, recv_sem).wait()
+
+    barrier = pltpu.get_barrier_semaphore()
+    peers = [device(x, y, moved(z, d, 8), core) for d in range(1, 8)]
+    peers += [device(moved(x, d), y, z, core) for d in range(1, 4)]
+    peers += [device(x, moved(y, d), z, core) for d in range(1, 4)]
+    peers += [device(x, y, z, 1 - core)]
+    for peer in peers:
+        pl.semaphore_signal(barrier, inc=1, device_id=peer, device_id_type=MESH)
+    here = out.at[x, lax.div(y, 2), core, z, lax.rem(y, 2)]
+    local_copy = pltpu.make_async_copy(own, here, copied)
+    local_copy.start()
+    pl.semaphore_wait(barrier, len(peers))
+
+    for d in (4, 3, 5, 2, 6, 1, 7):
+        send(own, here, z_send.at[d - 1], z_recv.at[d - 1], device(x, y, moved(z, d, 8), core))
+    local_copy.wait()
+    for d in (1, 7, 2, 6, 3, 5, 4):
+        arrived(out.at[x, lax.div(y, 2), core, moved(z, -d, 8), lax.rem(y, 2)], z_recv.at[d - 1])
+
+    def along(half, distance_first, distance_second):
+        if half == 0:
+            return moved(x, distance_first), moved(y, distance_second)
+        return moved(x, distance_second), moved(y, distance_first)
+
+    def to_core(half, j, k):
+        ref = piece(half, *along(half, j, k))
+        index = half * 16 + j * 4 + k
+        send(ref, ref, core_send.at[index], core_recv.at[index], device(x, y, z, 1 - core))
+
+    def to_second(half, j, k, e, slot):
+        ref = piece(half, *along(half, j, k))
+        index = half * 12 + slot * 4 + j
+        px, py = along(half, 0, e)
+        send(ref, ref, near_send.at[index], near_recv.at[index], device(px, py, z, core))
+
+    def first_arrived(half, d):
+        j = (4 - d) % 4
+        arrived(piece(half, *along(half, j, 0)), far_recv.at[half * 3 + d - 1])
+        to_second(half, j, 0, 1, 0)
+        to_second(half, j, 0, -1, 1)
+        to_core(half, j, 0)
+
+    def second_arrived(half, j, slot):
+        k = (3, 1, 2)[slot]
+        arrived(piece(half, *along(half, j, k)), near_recv.at[half * 12 + slot * 4 + j])
+        if slot == 0 and j in PLUS:
+            to_second(half, j, k, 1, 2)
+        if slot == 1 and j not in PLUS:
+            to_second(half, j, k, -1, 2)
+        to_core(half, j, k)
+
+    for half in range(2):
+        ref = piece(half, x, y)
+        for d in (1, 3, 2):
+            px, py = along(half, d, 0)
+            index = half * 3 + d - 1
+            send(ref, ref, far_send.at[index], far_recv.at[index], device(px, py, z, core))
+        to_second(half, 0, 0, 1, 0)
+        to_second(half, 0, 0, -1, 1)
+    for half in range(2):
+        to_core(half, 0, 0)
+    for d in (1, 3):
+        for half in range(2):
+            first_arrived(half, d)
+    for slot in (0, 1):
+        for half in range(2):
+            second_arrived(half, 0, slot)
+    for half in range(2):
+        first_arrived(half, 2)
+    for j in (3, 1, 2):
+        for slot in (0, 1):
+            for half in range(2):
+                second_arrived(half, j, slot)
+    for j in (0, 3, 1, 2):
+        for half in range(2):
+            second_arrived(half, j, 2)
+    for half in range(2):
+        for j in range(4):
+            for k in range(4):
+                px, py = along(half, j, k)
+                ref = out.at[px, lax.div(py, 2), 1 - core, pl.ds(4 * half, 4), lax.rem(py, 2)]
+                arrived(ref, core_recv.at[half * 16 + j * 4 + k])
+    for copy in started:
+        copy.wait_send()
+
+
+def gather(tiles):
+    def sems(count):
+        return pltpu.SemaphoreType.DMA((count,))
+
+    return pl.pallas_call(
+        gather_kernel,
+        out_shape=jax.ShapeDtypeStruct((4, 2, 2, 8, 2, 16, LANES), jnp.float32),
+        in_specs=[pl.BlockSpec(memory_space=pltpu.VMEM)],
+        out_specs=pl.BlockSpec(memory_space=pltpu.VMEM),
+        scratch_shapes=[
+            pltpu.SemaphoreType.DMA,
+            sems(7), sems(7), sems(6), sems(6), sems(24), sems(24), sems(32), sems(32),
+        ],
+        compiler_params=pltpu.CompilerParams(collective_id=0, has_side_effects=True),
+    )(tiles)
+
+
 def local(record):
     tiles = record.reshape(2, 8, LANES).transpose(1, 0, 2).reshape(16, LANES)
-    gathered = lax.all_gather(tiles, ("row", "col"), axis=0, tiled=True)
+    gathered = gather(tiles).reshape(2 * ROWS, LANES)
     result = spectra(gathered)
     result = result.reshape(WIDTH, WIDTH, WINDOWS, 2, 2, LANES)
     result = result.transpose(0, 1, 2, 4, 3, 5)

time: 753 us -> 45.6 us (0.06)
  waiting for transfers between devices: 722 us -> 0 us
  Pallas kernels: 14.9 us -> 45.4 us
  between operations: 13.4 us -> 0.01 us
    all_gather x1 -> x0, waiting for transfers between devices: 721 us -> none  [local(): gathered = lax.all_gather(tiles, ('row', 'col'), axis=0, tiled=True)]
    pallas_call x0 -> x1, Pallas kernels: none -> 30.5 us  [gather(): pl.pallas_call(gather_kernel, out_shape=jax.ShapeDtypeStruct((4, 2, 2, 8,...]
  transfers between devices with their start and end apart: 1 -> 0, of which waited for: 1 -> 0; matrix products, arithmetic and copies ran while one was open for 0% -> 0% of each run, Pallas kernels for 0% -> 0%
where the time goes in v2:
time: 45.6 us; the launch traced here: 45.4 us
  Pallas kernels  45.4 us (100%)
    pallas_call x1, Pallas kernels, gather(): pl.pallas_call(gather_kernel, out_shape=jax.ShapeDtypeStruct((4, 2, 2, 8,...  30.5 us
    pallas_call x1, Pallas kernels, spectra(): pl.pallas_call(kernel, grid=(WIDTH,), out_shape=jax.ShapeDtypeStruct((WID...  14.9 us

profile of v2, /device:TPU:1, one launch (start us, length us, event | category | flops | bytes accessed | tf_op | source)
XLA Modules:
  0.0 45.4 jit_solution(13693931462358134127)
XLA Ops:
  0.0 30.5 %shard_map.55 = f32[4,2,2,8,2,16,128]{6,5,4,3,2,1,0:T(8,128)} custom-call(f32[16,128]{1,0:T(8,128)} %bitcast.12), custom_call_target="tpu_custom_call" | custom-call | tf_op jit(solution)/shard_map/pallas_call | solution.py:284
  30.5 14.9 %shard_map.56 = f32[16384,128]{1,0:T(8,128)} custom-call(f32[4096,128]{1,0:T(8,128)} %bitcast.11, f32[2,768,128]{2,1,0:T(8,128)} %constant.8.clone.tables, f32[2,16,16,128]{3,2,1,0:T(8,128)} %constant.9.clone.turns, f32[128,128]{1,0:T(8,128)} %constant.10.clone.sign, bf16[2,2,256,256]{3,2,1,0:T(8,128)(2,1)} %constant.11.clone.second), custom_call_target="tpu_custom_call" | custom-call | tf_op jit(solution)/shard_map/pallas_call | solution.py:142

commit v3 on v2

--- a/solution.py
+++ b/solution.py
@@ -17,6 +17,9 @@
 ROWS = 2048
 PIECES = 3
 DEPTH = PIECES * 2 * LANES
+MESH = pl.DeviceIdType.MESH
+ORDER = (0, 1, 7, 2, 6, 3, 5, 4)
+SLOTS = 4
 
 
 def channel_tables():
@@ -74,7 +77,7 @@
     return lax.dot_general(a, b, (((1,), (0,)), ((), ())), preferred_element_type=jnp.float32)
 
 
-def channelize(gathered, tables, turns, sign, base):
+def first_weights(tables, turns, weights):
     row = lax.axis_index("row")
     col = lax.axis_index("col")
     lane = lax.broadcasted_iota(jnp.int32, (16, LANES), 1)
@@ -82,17 +85,36 @@
     sinus = jnp.where(lane < 64, turns[1, row], turns[1, col])
     groups = DEPTH // 16
     shaped = tables[...].reshape(2, groups, 16, LANES)
-    weights = (shaped[0] * cosine[None] + shaped[1] * sinus[None]).reshape(DEPTH, LANES)
-    high_w, low_w = halves(weights)
-    both = jnp.concatenate([high_w, low_w], axis=1)
+    full = (shaped[0] * cosine[None] + shaped[1] * sinus[None]).reshape(DEPTH, LANES)
+    high, low = halves(full)
+    weights[:, :LANES] = high
+    weights[:, LANES:] = low
+
+
+def in_order(held, ordered):
+    z = lax.div(lax.axis_index("col"), 2)
+
+    def window(w, _):
+        for o, d in enumerate(ORDER):
+            place = lax.rem(z + d, 8) * 32
+            for low in range(2):
+                block = held[lax.div(w, 4), lax.rem(lax.div(w, 2), 2) * 2 + low, lax.rem(w, 2), o]
+                ordered[pl.ds(pl.multiple_of(w * 256 + place + 16 * low, 16), 16), :] = block
+        return 0
+
+    lax.fori_loop(0, WINDOWS, window, 0)
+    ordered[2 * ROWS :, :] = jnp.zeros((8, LANES), jnp.float32)
+
+
+def channelize(ordered, weights, sign, base):
     step = 512
 
     def block(i, _):
         start = pl.multiple_of(i * (2 * step), 2 * step)
-        pieces = [gathered[pl.ds(start + j, step, stride=2), :] for j in range(2 * PIECES)]
+        pieces = [ordered[pl.ds(start + j, step, stride=2), :] for j in range(2 * PIECES)]
         high, low = halves(jnp.concatenate(pieces, axis=1))
-        wide = dot(high, both)
-        result = wide[:, :LANES] + wide[:, LANES:] + dot(low, high_w)
+        wide = dot(high, weights[...])
+        result = wide[:, :LANES] + wide[:, LANES:] + dot(low, weights[:, :LANES])
         for k in range(step // LANES):
             turned = result[k * LANES : (k + 1) * LANES].T * sign[...]
             base[pl.ds(i * (step // LANES) + k, LANES, stride=WINDOWS), :] = turned
@@ -121,49 +143,42 @@
         out[pl.ds(j, 256, stride=4), :] = value
 
 
-def kernel(gathered, tables, turns, sign, second, out, padded, base):
-    a = pl.program_id(0)
-
-    @pl.when(a == 0)
-    def _():
-        padded[0 : 2 * ROWS, :] = gathered[...]
-        padded[2 * ROWS :, :] = jnp.zeros((8, LANES), jnp.float32)
-        channelize(padded, tables, turns, sign, base)
-
-    correlate(a, base, second, out)
-
-
-def spectra(gathered):
-    tables, turns = channel_tables()
-
-    def whole(shape):
-        return pl.BlockSpec(shape, lambda a: (0,) * len(shape), pipeline_mode=pl.Buffered(1))
-
+def kernel(base, second, out, buffer, sems):
+    def store(a, slot):
+        place = pl.ds(pl.multiple_of(a * 1024, 1024), 1024)
+        return pltpu.make_async_copy(buffer.at[slot], out.at[place], sems.at[slot])
+
+    def step(a, _):
+        slot = lax.rem(a, SLOTS)
+
+        @pl.when(a >= SLOTS)
+        def _():
+            store(a, slot).wait()
+
+        correlate(a, base, second, buffer.at[slot])
+        store(a, slot).start()
+        return 0
+
+    lax.fori_loop(0, WIDTH, step, 0)
+    for a in range(WIDTH - SLOTS, WIDTH):
+        store(a, a % SLOTS).wait()
+
+
+def spectra(base):
+    whole = pl.BlockSpec(memory_space=pltpu.VMEM)
     return pl.pallas_call(
         kernel,
-        grid=(WIDTH,),
         out_shape=jax.ShapeDtypeStruct((WIDTH * 1024, LANES), jnp.float32),
-        in_specs=[
-            whole((2 * ROWS, LANES)),
-            whole((2, DEPTH, LANES)),
-            whole((2, 16, 16, LANES)),
-            whole((LANES, LANES)),
-            whole((2, 2, 256, 256)),
-        ],
-        out_specs=pl.BlockSpec((1024, LANES), lambda a: (a, 0)),
-        scratch_shapes=[
-            pltpu.VMEM((2 * ROWS + 8, LANES), jnp.float32),
-            pltpu.VMEM((LANES * WINDOWS, LANES), jnp.float32),
-        ],
-        compiler_params=pltpu.CompilerParams(dimension_semantics=("arbitrary",)),
-    )(gathered, jnp.asarray(tables), jnp.asarray(turns), jnp.asarray(signs()), jnp.asarray(second_tables()))
-
-
-MESH = pl.DeviceIdType.MESH
-PLUS = (0, 1)
-
-
-def gather_kernel(own, out, copied, z_send, z_recv, far_send, far_recv, near_send, near_recv, core_send, core_recv):
+        in_specs=[whole, whole],
+        out_specs=pl.BlockSpec(memory_space=pl.ANY),
+        scratch_shapes=[pltpu.VMEM((SLOTS, 1024, LANES), jnp.float32), pltpu.SemaphoreType.DMA((SLOTS,))],
+    )(base, jnp.asarray(second_tables()))
+
+
+def gather_kernel(
+    own, tables_hbm, turns_hbm, sign_hbm, base, out, ordered, tables, turns, sign, weights,
+    loaded, copied, z_send, z_recv, far_send, far_recv, near_send, near_recv, core_send, core_recv
+):
     row = lax.axis_index("row")
     col = lax.axis_index("col")
     core = lax.rem(row, 2)
@@ -178,7 +193,7 @@
         return lax.rem(value + (distance + length), length)
 
     def piece(half, x, y):
-        return out.at[x, lax.div(y, 2), core, pl.ds(4 * half, 4), lax.rem(y, 2)]
+        return out.at[x, y, core, pl.ds(4 * half, 4)]
 
     started = []
 
@@ -199,16 +214,24 @@
     peers += [device(x, y, z, 1 - core)]
     for peer in peers:
         pl.semaphore_signal(barrier, inc=1, device_id=peer, device_id_type=MESH)
-    here = out.at[x, lax.div(y, 2), core, z, lax.rem(y, 2)]
+    here = out.at[x, y, core, 0]
     local_copy = pltpu.make_async_copy(own, here, copied)
     local_copy.start()
+    loads = [
+        pltpu.make_async_copy(source, target, loaded.at[i])
+        for i, (source, target) in enumerate(((tables_hbm, tables), (turns_hbm, turns), (sign_hbm, sign)))
+    ]
+    for load in loads:
+        load.start()
     pl.semaphore_wait(barrier, len(peers))
 
-    for d in (4, 3, 5, 2, 6, 1, 7):
-        send(own, here, z_send.at[d - 1], z_recv.at[d - 1], device(x, y, moved(z, d, 8), core))
+    for o in range(1, 8):
+        target = out.at[x, y, core, o]
+        send(own, target, z_send.at[o - 1], z_recv.at[o - 1], device(x, y, moved(z, -ORDER[o], 8), core))
+    for load in loads:
+        load.wait()
+    first_weights(tables, turns, weights)
     local_copy.wait()
-    for d in (1, 7, 2, 6, 3, 5, 4):
-        arrived(out.at[x, lax.div(y, 2), core, moved(z, -d, 8), lax.rem(y, 2)], z_recv.at[d - 1])
 
     def along(half, distance_first, distance_second):
         if half == 0:
@@ -229,50 +252,59 @@
     def first_arrived(half, d):
         j = (4 - d) % 4
         arrived(piece(half, *along(half, j, 0)), far_recv.at[half * 3 + d - 1])
-        to_second(half, j, 0, 1, 0)
-        to_second(half, j, 0, -1, 1)
-        to_core(half, j, 0)
+        second_sent(half, j)
 
     def second_arrived(half, j, slot):
         k = (3, 1, 2)[slot]
         arrived(piece(half, *along(half, j, k)), near_recv.at[half * 12 + slot * 4 + j])
-        if slot == 0 and j in PLUS:
-            to_second(half, j, k, 1, 2)
-        if slot == 1 and j not in PLUS:
-            to_second(half, j, k, -1, 2)
         to_core(half, j, k)
 
-    for half in range(2):
+    def z_arrived(half):
+        for o in range(max(1, 4 * half), 4 * half + 4):
+            arrived(out.at[x, y, core, o], z_recv.at[o - 1])
+
+    def first_sent(half):
         ref = piece(half, x, y)
         for d in (1, 3, 2):
             px, py = along(half, d, 0)
             index = half * 3 + d - 1
             send(ref, ref, far_send.at[index], far_recv.at[index], device(px, py, z, core))
-        to_second(half, 0, 0, 1, 0)
-        to_second(half, 0, 0, -1, 1)
-    for half in range(2):
-        to_core(half, 0, 0)
-    for d in (1, 3):
-        for half in range(2):
+        second_sent(half, 0)
+
+    def second_sent(half, j):
+        to_second(half, j, 0, 1, 0)
+        to_second(half, j, 0, -1, 1)
+        to_second(half, j, 0, 2, 2)
+        to_core(half, j, 0)
+
+    z_arrived(0)
+    first_sent(0)
+    z_arrived(1)
+    first_sent(1)
+    for half in range(2):
+        for d in (1, 3):
             first_arrived(half, d)
-    for slot in (0, 1):
-        for half in range(2):
+        for slot in (0, 1):
             second_arrived(half, 0, slot)
     for half in range(2):
         first_arrived(half, 2)
-    for j in (3, 1, 2):
         for slot in (0, 1):
-            for half in range(2):
+            for j in (3, 1):
                 second_arrived(half, j, slot)
-    for j in (0, 3, 1, 2):
-        for half in range(2):
+    for half in range(2):
+        second_arrived(half, 0, 2)
+        for slot in (0, 1):
+            second_arrived(half, 2, slot)
+    for half in range(2):
+        for j in (3, 1, 2):
             second_arrived(half, j, 2)
     for half in range(2):
         for j in range(4):
             for k in range(4):
                 px, py = along(half, j, k)
-                ref = out.at[px, lax.div(py, 2), 1 - core, pl.ds(4 * half, 4), lax.rem(py, 2)]
-                arrived(ref, core_recv.at[half * 16 + j * 4 + k])
+                arrived(out.at[px, py, 1 - core, pl.ds(4 * half, 4)], core_recv.at[half * 16 + j * 4 + k])
+    in_order(out, ordered)
+    channelize(ordered, weights, sign, base)
     for copy in started:
         copy.wait_send()
 
@@ -281,23 +313,31 @@
     def sems(count):
         return pltpu.SemaphoreType.DMA((count,))
 
+    tables, turns = channel_tables()
+    anywhere = pl.BlockSpec(memory_space=pl.ANY)
     return pl.pallas_call(
         gather_kernel,
-        out_shape=jax.ShapeDtypeStruct((4, 2, 2, 8, 2, 16, LANES), jnp.float32),
-        in_specs=[pl.BlockSpec(memory_space=pltpu.VMEM)],
+        out_shape=jax.ShapeDtypeStruct((LANES * WINDOWS, LANES), jnp.float32),
+        in_specs=[pl.BlockSpec(memory_space=pltpu.VMEM), anywhere, anywhere, anywhere],
         out_specs=pl.BlockSpec(memory_space=pltpu.VMEM),
         scratch_shapes=[
+            pltpu.VMEM((4, 4, 2, 8, 16, LANES), jnp.float32),
+            pltpu.VMEM((2 * ROWS + 8, LANES), jnp.float32),
+            pltpu.VMEM(tables.shape, jnp.float32),
+            pltpu.VMEM(turns.shape, jnp.float32),
+            pltpu.VMEM((LANES, LANES), jnp.float32),
+            pltpu.VMEM((DEPTH, 2 * LANES), jnp.bfloat16),
+            sems(3),
             pltpu.SemaphoreType.DMA,
             sems(7), sems(7), sems(6), sems(6), sems(24), sems(24), sems(32), sems(32),
         ],
         compiler_params=pltpu.CompilerParams(collective_id=0, has_side_effects=True),
-    )(tiles)
+    )(tiles, jnp.asarray(tables), jnp.asarray(turns), jnp.asarray(signs()))
 
 
 def local(record):
     tiles = record.reshape(2, 8, LANES).transpose(1, 0, 2).reshape(16, LANES)
-    gathered = gather(tiles).reshape(2 * ROWS, LANES)
-    result = spectra(gathered)
+    result = spectra(gather(tiles))
     result = result.reshape(WIDTH, WIDTH, WINDOWS, 2, 2, LANES)
     result = result.transpose(0, 1, 2, 4, 3, 5)
     return result.reshape(WIDTH, WIDTH, WINDOWS, 2, 2 * LANES)

time: 45.6 us -> 41.9 us (0.919)
  Pallas kernels: 45.4 us -> 41.7 us
    pallas_call x2, Pallas kernels: 45.4 us -> 41.7 us  [the longest x1 33.1 us: gather(): pl.pallas_call(gather_kernel, out_shape=jax.ShapeDtypeStruct((LANES * WIN...]
where the time goes in v3:
time: 41.9 us; the launch traced here: 41.7 us
  Pallas kernels  41.7 us (100%)
    pallas_call x1, Pallas kernels, gather(): pl.pallas_call(gather_kernel, out_shape=jax.ShapeDtypeStruct((LANES * WIN...  33.1 us
    pallas_call x1, Pallas kernels, spectra(): pl.pallas_call(kernel, out_shape=jax.ShapeDtypeStruct((WIDTH * 1024, LANE...  8.58 us

profile of v3, /device:TPU:1, one launch (start us, length us, event | category | flops | bytes accessed | tf_op | source)
XLA Modules:
  0.0 41.7 jit_solution(9896741512335235884)
XLA Ops:
  0.0 33.1 %shard_map.55.base = f32[2048,128]{1,0:T(8,128)} custom-call(f32[16,128]{1,0:T(8,128)} %bitcast.10, f32[2,768,128]{2,1,0:T(8,128)} %constant.8.clone.tables_hbm, f32[2,16,16,128]{3,2,1,0:T(8,128)} %constant.9.clone.turns_hbm, f32[128,128]{1,0:T(8,128)} %constant.10.clone.sign_hbm), custom_call_target="tpu_custom_call" | custom-call | tf_op jit(solution)/shard_map/pallas_call | solution.py:318
  33.2 8.6 %shard_map.56 = f32[16384,128]{1,0:T(8,128)} custom-call(f32[2048,128]{1,0:T(8,128)} %shard_map.55.base, bf16[2,2,256,256]{3,2,1,0:T(8,128)(2,1)} %constant.11.clone.second), custom_call_target="tpu_custom_call" | custom-call | tf_op jit(solution)/shard_map/pallas_call | solution.py:169

commit v4 on v3

--- a/solution.py
+++ b/solution.py
@@ -18,7 +18,7 @@
 PIECES = 3
 DEPTH = PIECES * 2 * LANES
 MESH = pl.DeviceIdType.MESH
-ORDER = (0, 1, 7, 2, 6, 3, 5, 4)
+UNITS = ((0, 0), (1, 1), (7, 0), (2, 1), (6, 0), (3, 1), (5, 0), (4, 1))
 SLOTS = 4
 
 
@@ -91,21 +91,6 @@
     weights[:, LANES:] = low
 
 
-def in_order(held, ordered):
-    z = lax.div(lax.axis_index("col"), 2)
-
-    def window(w, _):
-        for o, d in enumerate(ORDER):
-            place = lax.rem(z + d, 8) * 32
-            for low in range(2):
-                block = held[lax.div(w, 4), lax.rem(lax.div(w, 2), 2) * 2 + low, lax.rem(w, 2), o]
-                ordered[pl.ds(pl.multiple_of(w * 256 + place + 16 * low, 16), 16), :] = block
-        return 0
-
-    lax.fori_loop(0, WINDOWS, window, 0)
-    ordered[2 * ROWS :, :] = jnp.zeros((8, LANES), jnp.float32)
-
-
 def channelize(ordered, weights, sign, base):
     step = 512
 
@@ -176,8 +161,8 @@
 
 
 def gather_kernel(
-    own, tables_hbm, turns_hbm, sign_hbm, base, out, ordered, tables, turns, sign, weights,
-    loaded, copied, z_send, z_recv, far_send, far_recv, near_send, near_recv, core_send, core_recv
+    own, tables_hbm, turns_hbm, sign_hbm, base, ordered, tables, turns, sign, weights,
+    loaded, copied, z_send, z_recv, first_send, first_recv, second_send, second_recv, core_send, core_recv
 ):
     row = lax.axis_index("row")
     col = lax.axis_index("col")
@@ -186,36 +171,45 @@
     y = lax.rem(lax.div(row, 2), 2) * 2 + lax.rem(col, 2)
     z = lax.div(col, 2)
 
+    def moved(value, distance, length=4):
+        return lax.rem(value + (distance + length), length) if distance else value
+
     def device(x, y, z, core):
         return (x * 4 + lax.div(y, 2) * 2 + core, z * 2 + lax.rem(y, 2))
 
-    def moved(value, distance, length=4):
-        return lax.rem(value + (distance + length), length)
-
-    def piece(half, x, y):
-        return out.at[x, y, core, pl.ds(4 * half, 4)]
-
-    started = []
-
-    def send(source, target, send_sem, recv_sem, to):
-        copy = pltpu.make_async_remote_copy(
-            src_ref=source, dst_ref=target, send_sem=send_sem, recv_sem=recv_sem, device_id=to, device_id_type=MESH
-        )
-        copy.start()
-        started.append(copy)
-
-    def arrived(ref, recv_sem):
-        pltpu.make_async_copy(ref, ref, recv_sem).wait()
+    def at(half, first, second):
+        px, py = ((first, second), (second, first))[half]
+        return moved(x, px), moved(y, py)
+
+    def beside(half, first, second):
+        return device(*at(half, first, second), z, core)
+
+    other = device(x, y, z, 1 - core)
+    x_rows = [moved(x, d) * 1024 for d in range(4)]
+    y_rows = [lax.div(moved(y, d), 2) * 512 + lax.rem(moved(y, d), 2) * 16 for d in range(4)]
+    z_rows = [moved(z, d, 8) * 32 + core * 256 for d in range(8)]
+
+    def chunk(unit, first, second):
+        d, half = UNITS[unit]
+        px, py = ((first, second), (second, first))[half]
+        return ordered.at[pl.ds(pl.multiple_of(x_rows[px % 4] + y_rows[py % 4] + z_rows[d], 16), 16)]
+
+    def send(ref, send_sem, recv_sem, to, source=None):
+        pltpu.make_async_remote_copy(
+            src_ref=ref if source is None else source,
+            dst_ref=ref, send_sem=send_sem, recv_sem=recv_sem, device_id=to, device_id_type=MESH,
+        ).start()
+
+    def wait(chunks, sem):
+        ref = ordered.at[pl.ds(0, 16 * chunks)]
+        pltpu.make_async_copy(ref, ref, sem).wait()
 
     barrier = pltpu.get_barrier_semaphore()
     peers = [device(x, y, moved(z, d, 8), core) for d in range(1, 8)]
-    peers += [device(moved(x, d), y, z, core) for d in range(1, 4)]
-    peers += [device(x, moved(y, d), z, core) for d in range(1, 4)]
-    peers += [device(x, y, z, 1 - core)]
+    peers += [beside(half, d, 0) for half in range(2) for d in range(1, 4)] + [other]
     for peer in peers:
         pl.semaphore_signal(barrier, inc=1, device_id=peer, device_id_type=MESH)
-    here = out.at[x, y, core, 0]
-    local_copy = pltpu.make_async_copy(own, here, copied)
+    local_copy = pltpu.make_async_copy(own, chunk(0, 0, 0), copied)
     local_copy.start()
     loads = [
         pltpu.make_async_copy(source, target, loaded.at[i])
@@ -223,90 +217,72 @@
     ]
     for load in loads:
         load.start()
+    ordered[2 * ROWS :, :] = jnp.zeros((8, LANES), jnp.float32)
     pl.semaphore_wait(barrier, len(peers))
 
-    for o in range(1, 8):
-        target = out.at[x, y, core, o]
-        send(own, target, z_send.at[o - 1], z_recv.at[o - 1], device(x, y, moved(z, -ORDER[o], 8), core))
+    def to_second(unit, j):
+        half = UNITS[unit][1]
+        for e in (1, 3, 2):
+            send(
+                chunk(unit, j, 0), second_send.at[unit], second_recv.at[unit * 3 + e - 1], beside(half, 0, e)
+            )
+
+    def to_core(unit, e):
+        for j in range(4):
+            send(chunk(unit, j, e), core_send.at[unit], core_recv.at[unit], other)
+
+    def begin(unit):
+        half = UNITS[unit][1]
+        for e in (1, 3, 2):
+            send(chunk(unit, 0, 0), first_send.at[unit], first_recv.at[unit], beside(half, e, 0))
+        to_second(unit, 0)
+
+    def z_done(unit):
+        wait(1, z_recv.at[unit - 1])
+        begin(unit)
+
+    def first_done(unit):
+        wait(3, first_recv.at[unit])
+        for j in (1, 3, 2):
+            to_second(unit, j)
+        to_core(unit, 0)
+
+    def second_done(unit):
+        for e in (1, 3, 2):
+            wait(4, second_recv.at[unit * 3 + e - 1])
+            to_core(unit, -e)
+
+    mine = x_rows[0] + y_rows[0] + z_rows[0]
+    for unit in range(1, 8):
+        d = UNITS[unit][0]
+        ref = ordered.at[pl.ds(pl.multiple_of(mine, 16), 16)]
+        send(ref, z_send.at[unit - 1], z_recv.at[unit - 1], device(x, y, moved(z, -d, 8), core), own)
+    local_copy.wait()
+    begin(0)
     for load in loads:
         load.wait()
     first_weights(tables, turns, weights)
-    local_copy.wait()
-
-    def along(half, distance_first, distance_second):
-        if half == 0:
-            return moved(x, distance_first), moved(y, distance_second)
-        return moved(x, distance_second), moved(y, distance_first)
-
-    def to_core(half, j, k):
-        ref = piece(half, *along(half, j, k))
-        index = half * 16 + j * 4 + k
-        send(ref, ref, core_send.at[index], core_recv.at[index], device(x, y, z, 1 - core))
-
-    def to_second(half, j, k, e, slot):
-        ref = piece(half, *along(half, j, k))
-        index = half * 12 + slot * 4 + j
-        px, py = along(half, 0, e)
-        send(ref, ref, near_send.at[index], near_recv.at[index], device(px, py, z, core))
-
-    def first_arrived(half, d):
-        j = (4 - d) % 4
-        arrived(piece(half, *along(half, j, 0)), far_recv.at[half * 3 + d - 1])
-        second_sent(half, j)
-
-    def second_arrived(half, j, slot):
-        k = (3, 1, 2)[slot]
-        arrived(piece(half, *along(half, j, k)), near_recv.at[half * 12 + slot * 4 + j])
-        to_core(half, j, k)
-
-    def z_arrived(half):
-        for o in range(max(1, 4 * half), 4 * half + 4):
-            arrived(out.at[x, y, core, o], z_recv.at[o - 1])
-
-    def first_sent(half):
-        ref = piece(half, x, y)
-        for d in (1, 3, 2):
-            px, py = along(half, d, 0)
-            index = half * 3 + d - 1
-            send(ref, ref, far_send.at[index], far_recv.at[index], device(px, py, z, core))
-        second_sent(half, 0)
-
-    def second_sent(half, j):
-        to_second(half, j, 0, 1, 0)
-        to_second(half, j, 0, -1, 1)
-        to_second(half, j, 0, 2, 2)
-        to_core(half, j, 0)
-
-    z_arrived(0)
-    first_sent(0)
-    z_arrived(1)
-    first_sent(1)
-    for half in range(2):
-        for d in (1, 3):
-            first_arrived(half, d)
-        for slot in (0, 1):
-            second_arrived(half, 0, slot)
-    for half in range(2):
-        first_arrived(half, 2)
-        for slot in (0, 1):
-            for j in (3, 1):
-                second_arrived(half, j, slot)
-    for half in range(2):
-        second_arrived(half, 0, 2)
-        for slot in (0, 1):
-            second_arrived(half, 2, slot)
-    for half in range(2):
-        for j in (3, 1, 2):
-            second_arrived(half, j, 2)
-    for half in range(2):
-        for j in range(4):
-            for k in range(4):
-                px, py = along(half, j, k)
-                arrived(out.at[px, py, 1 - core, pl.ds(4 * half, 4)], core_recv.at[half * 16 + j * 4 + k])
-    in_order(out, ordered)
+    z_done(1)
+    z_done(2)
+    first_done(0)
+    for unit in range(3, 8):
+        z_done(unit)
+    first_done(1)
+    first_done(2)
+    second_done(0)
+    for unit in range(3, 8):
+        first_done(unit)
+    for unit in range(1, 8):
+        second_done(unit)
+    for unit in range(8):
+        wait(16, core_recv.at[unit])
     channelize(ordered, weights, sign, base)
-    for copy in started:
-        copy.wait_send()
+    for unit in range(8):
+        if unit:
+            wait(1, z_send.at[unit - 1])
+        wait(3, first_send.at[unit])
+        wait(12, second_send.at[unit])
+        wait(16, core_send.at[unit])
 
 
 def gather(tiles):
@@ -321,7 +297,6 @@
         in_specs=[pl.BlockSpec(memory_space=pltpu.VMEM), anywhere, anywhere, anywhere],
         out_specs=pl.BlockSpec(memory_space=pltpu.VMEM),
         scratch_shapes=[
-            pltpu.VMEM((4, 4, 2, 8, 16, LANES), jnp.float32),
             pltpu.VMEM((2 * ROWS + 8, LANES), jnp.float32),
             pltpu.VMEM(tables.shape, jnp.float32),
             pltpu.VMEM(turns.shape, jnp.float32),
@@ -329,7 +304,7 @@
             pltpu.VMEM((DEPTH, 2 * LANES), jnp.bfloat16),
             sems(3),
             pltpu.SemaphoreType.DMA,
-            sems(7), sems(7), sems(6), sems(6), sems(24), sems(24), sems(32), sems(32),
+            sems(7), sems(7), sems(8), sems(8), sems(8), sems(24), sems(8), sems(8),
         ],
         compiler_params=pltpu.CompilerParams(collective_id=0, has_side_effects=True),
     )(tiles, jnp.asarray(tables), jnp.asarray(turns), jnp.asarray(signs()))

time: 41.9 us -> 38.9 us (0.928)
  Pallas kernels: 41.7 us -> 38.7 us
    pallas_call x1, Pallas kernels: 33.1 us -> 30.1 us  [gather(): pl.pallas_call(gather_kernel, out_shape=jax.ShapeDtypeStruct((LANES * WIN...]
where the time goes in v4:
time: 38.9 us; the launch traced here: 38.7 us
  Pallas kernels  38.7 us (99%)
    pallas_call x1, Pallas kernels, gather(): pl.pallas_call(gather_kernel, out_shape=jax.ShapeDtypeStruct((LANES * WIN...  30.1 us
    pallas_call x1, Pallas kernels, spectra(): pl.pallas_call(kernel, out_shape=jax.ShapeDtypeStruct((WIDTH * 1024, LANE...  8.58 us

profile of v4, /device:TPU:1, one launch (start us, length us, event | category | flops | bytes accessed | tf_op | source)
XLA Modules:
  0.0 38.7 jit_solution(13114933677381904934)
XLA Ops:
  0.0 30.1 %shard_map.55.base = f32[2048,128]{1,0:T(8,128)} custom-call(f32[16,128]{1,0:T(8,128)} %bitcast.10, f32[2,768,128]{2,1,0:T(8,128)} %constant.8.clone.tables_hbm, f32[2,16,16,128]{3,2,1,0:T(8,128)} %constant.9.clone.turns_hbm, f32[128,128]{1,0:T(8,128)} %constant.10.clone.sign_hbm), custom_call_target="tpu_custom_call" | custom-call | tf_op jit(solution)/shard_map/pallas_call | solution.py:294
  30.1 8.6 %shard_map.56 = f32[16384,128]{1,0:T(8,128)} custom-call(f32[2048,128]{1,0:T(8,128)} %shard_map.55.base, bf16[2,2,256,256]{3,2,1,0:T(8,128)(2,1)} %constant.11.clone.second), custom_call_target="tpu_custom_call" | custom-call | tf_op jit(solution)/shard_map/pallas_call | solution.py:154

commit v5 on v4

--- a/solution.py
+++ b/solution.py
@@ -20,51 +20,29 @@
 MESH = pl.DeviceIdType.MESH
 UNITS = ((0, 0), (1, 1), (7, 0), (2, 1), (6, 0), (3, 1), (5, 0), (4, 1))
 SLOTS = 4
-
-
-def channel_tables():
-    position = np.arange(PIECES * LANES)
-    table = np.zeros((PIECES, 2, LANES, 2, 2, WIDTH))
-    turned = np.zeros_like(table)
-    for parity in range(2):
-        m = position - HOP * parity
-        inside = (m >= 0) & (m < C)
-        hann = np.where(inside, (0.5 - 0.5 * np.cos(2 * np.pi * m / C)) / math.sqrt(3 * C / 8), 0.0)
-        turns = (position[:, None] * np.arange(WIDTH)[None]) % C
-        w = hann[:, None] * np.exp(-2j * np.pi * turns / C)
-        for part, v in enumerate((w, 1j * w)):
-            v = v.reshape(PIECES, LANES, WIDTH)
-            table[:, part, :, parity, 0] = v.real
-            table[:, part, :, parity, 1] = v.imag
-            turned[:, part, :, parity, 0] = v.imag
-            turned[:, part, :, parity, 1] = -v.real
-    tables = np.stack([table, turned]).reshape(2, DEPTH, 64)
-    tables = np.concatenate([tables, tables], axis=2)
-    angle = 2 * np.pi * (np.arange(16)[:, None] * np.arange(16)[None] % 16) / 16
-    turns = np.stack([np.cos(angle), np.sin(angle)])
-    turns = np.broadcast_to(turns[..., None], (2, 16, 16, LANES))
-    return tables.astype(np.float32), np.ascontiguousarray(turns).astype(np.float32)
-
-
-def second_tables():
-    frame = np.arange(LANES)
-    bins = np.arange(LANES)
-    out = []
-    for parity in range(2):
-        turns = ((2 * frame[:, None] + parity) * bins[None]) % P_SIZE
-        angle = 2 * np.pi * turns / P_SIZE
-        c, s = np.cos(angle) / 16.0, np.sin(angle) / 16.0
-        out.append(np.concatenate([np.concatenate([c, -s], 1), np.concatenate([s, c], 1)], 0))
-    full = np.stack(out).astype(np.float32)
-    high = full.astype(jnp.bfloat16)
-    low = (full - high.astype(np.float32)).astype(jnp.bfloat16)
-    return np.stack([high, low])
-
-
-def signs():
-    channel = np.arange(LANES) % WIDTH
-    frame = np.arange(LANES)
-    return np.where((channel[:, None] * frame[None]) % 2 == 1, -1.0, 1.0).astype(np.float32)
+VMEM_LIMIT = 16 * 2**20
+
+
+def cosine_series():
+    nodes = 0.5 - 0.5 * np.cos(np.pi * (np.arange(64) + 0.5) / 64)
+    fit = np.polynomial.chebyshev.Chebyshev.fit(nodes, -np.cos(np.pi * np.sqrt(nodes)), 8, domain=[0, 1])
+    return [float(c) for c in fit.convert(kind=np.polynomial.Polynomial).coef]
+
+
+SERIES = cosine_series()
+
+
+def cosine(turns):
+    w = ((turns & 255) - 128).astype(jnp.float32) * (1.0 / 128)
+    square = w * w
+    result = jnp.full(w.shape, SERIES[-1], jnp.float32)
+    for c in SERIES[-2::-1]:
+        result = result * square + c
+    return result
+
+
+def grid_of(dim):
+    return lax.broadcasted_iota(jnp.int32, (LANES, LANES), dim)
 
 
 def halves(value):
@@ -77,22 +55,42 @@
     return lax.dot_general(a, b, (((1,), (0,)), ((), ())), preferred_element_type=jnp.float32)
 
 
-def first_weights(tables, turns, weights):
-    row = lax.axis_index("row")
-    col = lax.axis_index("col")
-    lane = lax.broadcasted_iota(jnp.int32, (16, LANES), 1)
-    cosine = jnp.where(lane < 64, turns[0, row], turns[0, col])
-    sinus = jnp.where(lane < 64, turns[1, row], turns[1, col])
-    groups = DEPTH // 16
-    shaped = tables[...].reshape(2, groups, 16, LANES)
-    full = (shaped[0] * cosine[None] + shaped[1] * sinus[None]).reshape(DEPTH, LANES)
-    high, low = halves(full)
-    weights[:, :LANES] = high
-    weights[:, LANES:] = low
-
-
-def channelize(ordered, weights, sign, base):
+def first_weights(weights):
+    column = grid_of(1)
+    block = jnp.where(column < 64, lax.axis_index("row"), lax.axis_index("col"))
+    channel = block * WIDTH + column % WIDTH
+    odd = (column // 32) % 2
+    imag = (column // 16) % 2
+    for piece in range(PIECES):
+        position = grid_of(0) + piece * LANES
+        m = position - HOP * odd
+        window = (0.5 - 0.5 * cosine(m)) * (1.0 / math.sqrt(3 * C / 8))
+        window = jnp.where((m >= 0) & (m < C), window, 0.0)
+        for part in range(2):
+            shift = 64 * imag if part == 0 else 192 * (1 - imag)
+            high, low = halves(window * cosine(channel * position + shift))
+            start = (2 * piece + part) * LANES
+            weights[start : start + LANES, :LANES] = high
+            weights[start : start + LANES, LANES:] = low
+
+
+def second_tables(second):
+    for parity in range(2):
+        turns = (2 * grid_of(0) + parity) * grid_of(1)
+        plain = cosine(turns) * (1.0 / 16)
+        for part in range(2):
+            for imag in range(2):
+                value = plain if part == imag else cosine(turns + (64 if imag else 192)) * (1.0 / 16)
+                high, low = halves(value)
+                rows = slice(part * LANES, (part + 1) * LANES)
+                columns = slice(imag * LANES, (imag + 1) * LANES)
+                second[0, parity, rows, columns] = high
+                second[1, parity, rows, columns] = low
+
+
+def channelize(ordered, weights, base):
     step = 512
+    sign = (1 - 2 * (grid_of(0) & grid_of(1) & 1)).astype(jnp.float32)
 
     def block(i, _):
         start = pl.multiple_of(i * (2 * step), 2 * step)
@@ -101,7 +99,7 @@
         wide = dot(high, weights[...])
         result = wide[:, :LANES] + wide[:, LANES:] + dot(low, weights[:, :LANES])
         for k in range(step // LANES):
-            turned = result[k * LANES : (k + 1) * LANES].T * sign[...]
+            turned = result[k * LANES : (k + 1) * LANES].T * sign
             base[pl.ds(i * (step // LANES) + k, LANES, stride=WINDOWS), :] = turned
         return 0
 
@@ -149,7 +147,7 @@
         store(a, a % SLOTS).wait()
 
 
-def spectra(base):
+def spectra(base, second):
     whole = pl.BlockSpec(memory_space=pltpu.VMEM)
     return pl.pallas_call(
         kernel,
@@ -157,12 +155,13 @@
         in_specs=[whole, whole],
         out_specs=pl.BlockSpec(memory_space=pl.ANY),
         scratch_shapes=[pltpu.VMEM((SLOTS, 1024, LANES), jnp.float32), pltpu.SemaphoreType.DMA((SLOTS,))],
-    )(base, jnp.asarray(second_tables()))
+        compiler_params=pltpu.CompilerParams(vmem_limit_bytes=VMEM_LIMIT),
+    )(base, second)
 
 
 def gather_kernel(
-    own, tables_hbm, turns_hbm, sign_hbm, base, ordered, tables, turns, sign, weights,
-    loaded, copied, z_send, z_recv, first_send, first_recv, second_send, second_recv, core_send, core_recv
+    own, base, second, ordered, weights, copied,
+    z_send, z_recv, first_send, first_recv, second_send, second_recv, core_send, core_recv
 ):
     row = lax.axis_index("row")
     col = lax.axis_index("col")
@@ -194,10 +193,9 @@
         px, py = ((first, second), (second, first))[half]
         return ordered.at[pl.ds(pl.multiple_of(x_rows[px % 4] + y_rows[py % 4] + z_rows[d], 16), 16)]
 
-    def send(ref, send_sem, recv_sem, to, source=None):
+    def send(ref, send_sem, recv_sem, to):
         pltpu.make_async_remote_copy(
-            src_ref=ref if source is None else source,
-            dst_ref=ref, send_sem=send_sem, recv_sem=recv_sem, device_id=to, device_id_type=MESH,
+            src_ref=ref, dst_ref=ref, send_sem=send_sem, recv_sem=recv_sem, device_id=to, device_id_type=MESH
         ).start()
 
     def wait(chunks, sem):
@@ -211,12 +209,6 @@
         pl.semaphore_signal(barrier, inc=1, device_id=peer, device_id_type=MESH)
     local_copy = pltpu.make_async_copy(own, chunk(0, 0, 0), copied)
     local_copy.start()
-    loads = [
-        pltpu.make_async_copy(source, target, loaded.at[i])
-        for i, (source, target) in enumerate(((tables_hbm, tables), (turns_hbm, turns), (sign_hbm, sign)))
-    ]
-    for load in loads:
-        load.start()
     ordered[2 * ROWS :, :] = jnp.zeros((8, LANES), jnp.float32)
     pl.semaphore_wait(barrier, len(peers))
 
@@ -253,20 +245,19 @@
             to_core(unit, -e)
 
     mine = x_rows[0] + y_rows[0] + z_rows[0]
+    local_copy.wait()
     for unit in range(1, 8):
         d = UNITS[unit][0]
         ref = ordered.at[pl.ds(pl.multiple_of(mine, 16), 16)]
-        send(ref, z_send.at[unit - 1], z_recv.at[unit - 1], device(x, y, moved(z, -d, 8), core), own)
-    local_copy.wait()
+        send(ref, z_send.at[unit - 1], z_recv.at[unit - 1], device(x, y, moved(z, -d, 8), core))
     begin(0)
-    for load in loads:
-        load.wait()
-    first_weights(tables, turns, weights)
+    first_weights(weights)
     z_done(1)
     z_done(2)
     first_done(0)
     for unit in range(3, 8):
         z_done(unit)
+    second_tables(second)
     first_done(1)
     first_done(2)
     second_done(0)
@@ -276,7 +267,7 @@
         second_done(unit)
     for unit in range(8):
         wait(16, core_recv.at[unit])
-    channelize(ordered, weights, sign, base)
+    channelize(ordered, weights, base)
     for unit in range(8):
         if unit:
             wait(1, z_send.at[unit - 1])
@@ -289,30 +280,31 @@
     def sems(count):
         return pltpu.SemaphoreType.DMA((count,))
 
-    tables, turns = channel_tables()
-    anywhere = pl.BlockSpec(memory_space=pl.ANY)
+    far = pl.BlockSpec(memory_space=pl.ANY)
+    near = pl.BlockSpec(memory_space=pltpu.VMEM)
     return pl.pallas_call(
         gather_kernel,
-        out_shape=jax.ShapeDtypeStruct((LANES * WINDOWS, LANES), jnp.float32),
-        in_specs=[pl.BlockSpec(memory_space=pltpu.VMEM), anywhere, anywhere, anywhere],
-        out_specs=pl.BlockSpec(memory_space=pltpu.VMEM),
+        out_shape=[
+            jax.ShapeDtypeStruct((LANES * WINDOWS, LANES), jnp.float32),
+            jax.ShapeDtypeStruct((2, 2, 256, 256), jnp.bfloat16),
+        ],
+        in_specs=[far],
+        out_specs=[near] * 2,
         scratch_shapes=[
             pltpu.VMEM((2 * ROWS + 8, LANES), jnp.float32),
-            pltpu.VMEM(tables.shape, jnp.float32),
-            pltpu.VMEM(turns.shape, jnp.float32),
-            pltpu.VMEM((LANES, LANES), jnp.float32),
             pltpu.VMEM((DEPTH, 2 * LANES), jnp.bfloat16),
-            sems(3),
             pltpu.SemaphoreType.DMA,
             sems(7), sems(7), sems(8), sems(8), sems(8), sems(24), sems(8), sems(8),
         ],
-        compiler_params=pltpu.CompilerParams(collective_id=0, has_side_effects=True),
-    )(tiles, jnp.asarray(tables), jnp.asarray(turns), jnp.asarray(signs()))
+        compiler_params=pltpu.CompilerParams(
+            collective_id=0, has_side_effects=True, vmem_limit_bytes=VMEM_LIMIT
+        ),
+    )(tiles)
 
 
 def local(record):
     tiles = record.reshape(2, 8, LANES).transpose(1, 0, 2).reshape(16, LANES)
-    result = spectra(gather(tiles))
+    result = spectra(*gather(tiles))
     result = result.reshape(WIDTH, WIDTH, WINDOWS, 2, 2, LANES)
     result = result.transpose(0, 1, 2, 4, 3, 5)
     return result.reshape(WIDTH, WIDTH, WINDOWS, 2, 2 * LANES)

time: 38.9 us -> 36.5 us (0.938)
  Pallas kernels: 38.7 us -> 35.7 us
  local copies, waits for them, and re-layouts: 0 us -> 0.7 us
    pallas_call x1, Pallas kernels: 30.1 us -> 28.5 us  [gather(): pl.pallas_call(gather_kernel, out_shape=[jax.ShapeDtypeStruct((LANES * WI...]
    pallas_call x1, Pallas kernels: 8.58 us -> 7.23 us  [spectra(): pl.pallas_call(kernel, out_shape=jax.ShapeDtypeStruct((WIDTH * 1024, LANE...]
    unnamed x0 -> x2, local copies, waits for them, and re-layouts: none -> 0.7 us
where the time goes in v5:
time: 36.5 us; the launch traced here: 36.4 us
  Pallas kernels  35.7 us (98%)
  local copies, waits for them, and re-layouts  0.7 us (2%)
    pallas_call x1, Pallas kernels, gather(): pl.pallas_call(gather_kernel, out_shape=[jax.ShapeDtypeStruct((LANES * WI...  28.5 us
    pallas_call x1, Pallas kernels, spectra(): pl.pallas_call(kernel, out_shape=jax.ShapeDtypeStruct((WIDTH * 1024, LANE...  7.23 us

profile of v5, /device:TPU:1, one launch (start us, length us, event | category | flops | bytes accessed | tf_op | source)
XLA Modules:
  0.0 36.4 jit_solution(2340885730801827275)
XLA Ops:
  0.0 0.0 copy-start
  0.0 0.7 %copy-done = f32[2,1024]{1,0:T(2,128)S(1)} copy-done((f32[2,1024]{1,0:T(2,128)S(1)}, f32[2,1024]{1,0:T(2,128)}, u32[]{:S(2)}) %copy-start) | copy-done | bytes 8216
  0.7 28.5 %shard_map.17 = (f32[2048,128]{1,0:T(8,128)S(1)}, bf16[2,2,256,256]{3,2,1,0:T(8,128)(2,1)S(1)}) custom-call(f32[16,128]{1,0:T(8,128)S(1)} %bitcast.10), custom_call_target="tpu_custom_call" | custom-call | tf_op jit(solution)/shard_map/pallas_call | solution.py:285
  29.2 7.2 %shard_map.18 = f32[16384,128]{1,0:T(8,128)} custom-call(f32[2048,128]{1,0:T(8,128)S(1)} %get-tuple-element.7.base, bf16[2,2,256,256]{3,2,1,0:T(8,128)(2,1)S(1)} %get-tuple-element.8.second), custom_call_target="tpu_custom_call" | custom-call | tf_op jit(solution)/shard_map/pallas_call | solution.py:152
Async XLA Ops:
  0.0 0.7 %copy-start = (f32[2,1024]{1,0:T(2,128)S(1)}, f32[2,1024]{1,0:T(2,128)}, u32[]{:S(2)}) copy-start(f32[2,1024]{1,0:T(2,128)} %param.1) | copy-start | bytes 24580

commit v6 on v5

--- a/solution.py
+++ b/solution.py
@@ -20,6 +20,7 @@
 MESH = pl.DeviceIdType.MESH
 UNITS = ((0, 0), (1, 1), (7, 0), (2, 1), (6, 0), (3, 1), (5, 0), (4, 1))
 SLOTS = 4
+GROUP = 4
 VMEM_LIMIT = 16 * 2**20
 
 
@@ -106,29 +107,35 @@
     lax.fori_loop(0, ROWS // step, block, 0)
 
 
-def correlate(a, base, second, out):
-    def tile(first, count):
-        return base[pl.ds(pl.multiple_of(first * WINDOWS, WINDOWS), count * WINDOWS), :]
+def correlate(step, base, second, out):
+    count = GROUP * 256
+
+    def tile(first, channels):
+        return base[pl.ds(pl.multiple_of(first * WINDOWS, WINDOWS), channels * WINDOWS), :]
 
     sums = []
     for parity in range(2):
-        lead_re = tile(parity * 32 + a, 1)[None]
-        lead_im = tile(parity * 32 + 16 + a, 1)[None]
-        trail_re = tile(64 + parity * 32, 16).reshape(WIDTH, WINDOWS, LANES)
-        trail_im = tile(64 + parity * 32 + 16, 16).reshape(WIDTH, WINDOWS, LANES)
-        real = (lead_re * trail_re + lead_im * trail_im).reshape(256, LANES)
-        imag = (lead_im * trail_re - lead_re * trail_im).reshape(256, LANES)
+        lead_re = tile(parity * 32 + step * GROUP, GROUP).reshape(GROUP, 1, WINDOWS, LANES)
+        lead_im = tile(parity * 32 + 16 + step * GROUP, GROUP).reshape(GROUP, 1, WINDOWS, LANES)
+        trail_re = tile(64 + parity * 32, 16).reshape(1, WIDTH, WINDOWS, LANES)
+        trail_im = tile(64 + parity * 32 + 16, 16).reshape(1, WIDTH, WINDOWS, LANES)
+        real = (lead_re * trail_re + lead_im * trail_im).reshape(count, LANES)
+        imag = (lead_im * trail_re - lead_re * trail_im).reshape(count, LANES)
         high, low = halves(jnp.concatenate([real, imag], axis=1))
-        sums.append(dot(high, second[0, parity]) + dot(low, second[0, parity]) + dot(high, second[1, parity]))
+        both = dot(jnp.concatenate([high, low], axis=0), second[0, parity])
+        sums.append(both[:count] + both[count:] + dot(high, second[1, parity]))
     total = sums[0] + sums[1]
     rest = sums[0] - sums[1]
     for j, value in enumerate((total[:, :LANES], total[:, LANES:], rest[:, :LANES], rest[:, LANES:])):
-        out[pl.ds(j, 256, stride=4), :] = value
+        out[pl.ds(j, count, stride=4), :] = value
 
 
 def kernel(base, second, out, buffer, sems):
+    size = GROUP * 1024
+    steps = WIDTH // GROUP
+
     def store(a, slot):
-        place = pl.ds(pl.multiple_of(a * 1024, 1024), 1024)
+        place = pl.ds(pl.multiple_of(a * size, size), size)
         return pltpu.make_async_copy(buffer.at[slot], out.at[place], sems.at[slot])
 
     def step(a, _):
@@ -142,8 +149,8 @@
         store(a, slot).start()
         return 0
 
-    lax.fori_loop(0, WIDTH, step, 0)
-    for a in range(WIDTH - SLOTS, WIDTH):
+    lax.fori_loop(0, steps, step, 0)
+    for a in range(steps - SLOTS, steps):
         store(a, a % SLOTS).wait()
 
 
@@ -154,7 +161,7 @@
         out_shape=jax.ShapeDtypeStruct((WIDTH * 1024, LANES), jnp.float32),
         in_specs=[whole, whole],
         out_specs=pl.BlockSpec(memory_space=pl.ANY),
-        scratch_shapes=[pltpu.VMEM((SLOTS, 1024, LANES), jnp.float32), pltpu.SemaphoreType.DMA((SLOTS,))],
+        scratch_shapes=[pltpu.VMEM((SLOTS, GROUP * 1024, LANES), jnp.float32), pltpu.SemaphoreType.DMA((SLOTS,))],
         compiler_params=pltpu.CompilerParams(vmem_limit_bytes=VMEM_LIMIT),
     )(base, second)
 
@@ -280,7 +287,7 @@
     def sems(count):
         return pltpu.SemaphoreType.DMA((count,))
 
-    far = pl.BlockSpec(memory_space=pl.ANY)
+    far = pl.BlockSpec(memory_space=pltpu.HBM)
     near = pl.BlockSpec(memory_space=pltpu.VMEM)
     return pl.pallas_call(
         gather_kernel,
@@ -304,6 +311,7 @@
 
 def local(record):
     tiles = record.reshape(2, 8, LANES).transpose(1, 0, 2).reshape(16, LANES)
+    tiles = pltpu.with_memory_space_constraint(tiles, pltpu.HBM)
     result = spectra(*gather(tiles))
     result = result.reshape(WIDTH, WIDTH, WINDOWS, 2, 2, LANES)
     result = result.transpose(0, 1, 2, 4, 3, 5)

time: 36.5 us -> 33.9 us (0.929)
  Pallas kernels: 35.7 us -> 33.8 us
  local copies, waits for them, and re-layouts: 0.7 us -> 0 us
    pallas_call x1, Pallas kernels: 7.23 us -> 5.35 us  [spectra(): pl.pallas_call(kernel, out_shape=jax.ShapeDtypeStruct((WIDTH * 1024, LANE...]
    unnamed x2 -> x0, local copies, waits for them, and re-layouts: 0.7 us -> none
where the time goes in v6:
time: 33.9 us; the launch traced here: 33.8 us
  Pallas kernels  33.8 us (100%)
    pallas_call x1, Pallas kernels, gather(): pl.pallas_call(gather_kernel, out_shape=[jax.ShapeDtypeStruct((LANES * WI...  28.5 us
    pallas_call x1, Pallas kernels, spectra(): pl.pallas_call(kernel, out_shape=jax.ShapeDtypeStruct((WIDTH * 1024, LANE...  5.35 us

profile of v6, /device:TPU:1, one launch (start us, length us, event | category | flops | bytes accessed | tf_op | source)
XLA Modules:
  0.0 33.8 jit_solution(4129735050195074385)
XLA Ops:
  0.0 28.5 %shard_map.17 = (f32[2048,128]{1,0:T(8,128)S(1)}, bf16[2,2,256,256]{3,2,1,0:T(8,128)(2,1)S(1)}) custom-call(f32[16,128]{1,0:T(8,128)} %bitcast.10), custom_call_target="tpu_custom_call" | custom-call | tf_op jit(solution)/shard_map/pallas_call | solution.py:292
  28.5 5.3 %shard_map.18 = f32[16384,128]{1,0:T(8,128)} custom-call(f32[2048,128]{1,0:T(8,128)S(1)} %get-tuple-element.7.base, bf16[2,2,256,256]{3,2,1,0:T(8,128)(2,1)S(1)} %get-tuple-element.8.second), custom_call_target="tpu_custom_call" | custom-call | tf_op jit(solution)/shard_map/pallas_call | solution.py:159

commit v7 on v6

--- a/solution.py
+++ b/solution.py
@@ -90,15 +90,15 @@
 
 
 def channelize(ordered, weights, base):
-    step = 512
+    step = 1024
     sign = (1 - 2 * (grid_of(0) & grid_of(1) & 1)).astype(jnp.float32)
 
     def block(i, _):
         start = pl.multiple_of(i * (2 * step), 2 * step)
         pieces = [ordered[pl.ds(start + j, step, stride=2), :] for j in range(2 * PIECES)]
         high, low = halves(jnp.concatenate(pieces, axis=1))
-        wide = dot(high, weights[...])
-        result = wide[:, :LANES] + wide[:, LANES:] + dot(low, weights[:, :LANES])
+        wide = dot(jnp.concatenate([high, low], axis=0), weights[...])
+        result = wide[:step, :LANES] + wide[:step, LANES:] + wide[step:, :LANES]
         for k in range(step // LANES):
             turned = result[k * LANES : (k + 1) * LANES].T * sign
             base[pl.ds(i * (step // LANES) + k, LANES, stride=WINDOWS), :] = turned
@@ -149,7 +149,7 @@
         store(a, slot).start()
         return 0
 
-    lax.fori_loop(0, steps, step, 0)
+    lax.fori_loop(0, steps, step, 0, unroll=True)
     for a in range(steps - SLOTS, steps):
         store(a, a % SLOTS).wait()
 

time: 33.9 us -> 32.9 us (0.971)
  Pallas kernels: 33.8 us -> 32.9 us
    pallas_call x1, Pallas kernels: 28.5 us -> 27.9 us  [gather(): pl.pallas_call(gather_kernel, out_shape=[jax.ShapeDtypeStruct((LANES * WI...]
    pallas_call x1, Pallas kernels: 5.35 us -> 4.92 us  [spectra(): pl.pallas_call(kernel, out_shape=jax.ShapeDtypeStruct((WIDTH * 1024, LANE...]
where the time goes in v7:
time: 32.9 us
  Pallas kernels  32.9 us (100%)
    pallas_call x1, Pallas kernels, gather(): pl.pallas_call(gather_kernel, out_shape=[jax.ShapeDtypeStruct((LANES * WI...  27.9 us
    pallas_call x1, Pallas kernels, spectra(): pl.pallas_call(kernel, out_shape=jax.ShapeDtypeStruct((WIDTH * 1024, LANE...  4.92 us

profile of v7, /device:TPU:1, one launch (start us, length us, event | category | flops | bytes accessed | tf_op | source)
XLA Modules:
  0.0 32.9 jit_solution(5423942075424290431)
XLA Ops:
  0.0 27.9 %shard_map.17 = (f32[2048,128]{1,0:T(8,128)S(1)}, bf16[2,2,256,256]{3,2,1,0:T(8,128)(2,1)S(1)}) custom-call(f32[16,128]{1,0:T(8,128)} %bitcast.10), custom_call_target="tpu_custom_call" | custom-call | tf_op jit(solution)/shard_map/pallas_call | solution.py:292
  28.0 4.9 %shard_map.18 = f32[16384,128]{1,0:T(8,128)} custom-call(f32[2048,128]{1,0:T(8,128)S(1)} %get-tuple-element.7.base, bf16[2,2,256,256]{3,2,1,0:T(8,128)(2,1)S(1)} %get-tuple-element.8.second), custom_call_target="tpu_custom_call" | custom-call | tf_op jit(solution)/shard_map/pallas_call | solution.py:159

commit v8 on v7

--- a/solution.py
+++ b/solution.py
@@ -104,7 +104,7 @@
             base[pl.ds(i * (step // LANES) + k, LANES, stride=WINDOWS), :] = turned
         return 0
 
-    lax.fori_loop(0, ROWS // step, block, 0)
+    lax.fori_loop(0, ROWS // step, block, 0, unroll=True)
 
 
 def correlate(step, base, second, out):

time: 32.9 us -> 32.8 us (level)
  no operation moved by 1% of the time
where the time goes in v8:
time: 32.8 us; the launch traced here: 32.7 us
  Pallas kernels  32.7 us (100%)
    pallas_call x1, Pallas kernels, gather(): pl.pallas_call(gather_kernel, out_shape=[jax.ShapeDtypeStruct((LANES * WI...  27.8 us
    pallas_call x1, Pallas kernels, spectra(): pl.pallas_call(kernel, out_shape=jax.ShapeDtypeStruct((WIDTH * 1024, LANE...  4.92 us

profile of v8, /device:TPU:1, one launch (start us, length us, event | category | flops | bytes accessed | tf_op | source)
XLA Modules:
  0.0 32.7 jit_solution(7887429390015297844)
XLA Ops:
  0.0 27.8 %shard_map.17 = (f32[2048,128]{1,0:T(8,128)S(1)}, bf16[2,2,256,256]{3,2,1,0:T(8,128)(2,1)S(1)}) custom-call(f32[16,128]{1,0:T(8,128)} %bitcast.10), custom_call_target="tpu_custom_call" | custom-call | tf_op jit(solution)/shard_map/pallas_call | solution.py:292
  27.8 4.9 %shard_map.18 = f32[16384,128]{1,0:T(8,128)} custom-call(f32[2048,128]{1,0:T(8,128)S(1)} %get-tuple-element.7.base, bf16[2,2,256,256]{3,2,1,0:T(8,128)(2,1)S(1)} %get-tuple-element.8.second), custom_call_target="tpu_custom_call" | custom-call | tf_op jit(solution)/shard_map/pallas_call | solution.py:159
